TPU v7x, 512 devices: a whole 4x4x16 slice. The times are simulated.
512 devices in a mesh: pool: 32 (over z, y_hi), band: 16 (over y_lo, x, core).
Axes of the slice: x: 4, y: 4 (y_hi: 2, y_lo: 2; y = y_hi * 2 + y_lo), z: 16, core: 2. Of those that a mesh axis runs over, the one named last changes fastest.
Arguments:
- orbitals: bfloat16 [32, 16, 2, 46656], P('pool', 'band'), may hold values from -6 to 6
- occupation: int32 [32, 16], P('pool', 'band'), may hold values from 1 to 2
- kernel: float32 [46656], replicated, may hold values from 0.02 to 2
Outputs:
- exchanged: bfloat16 [32, 16, 2, 46656], P('pool', 'band')
- gram_matrix: float32 [32, 2, 16, 16], P('pool', None, None, 'band')
All inputs are finite; a program needn't handle non-finite values.
Results may differ from a plain program's by a relative error of at most 0.013.
Values may be sent and summed in bfloat16 or wider, within the bound.
A program may use at most 64 MiB of HBM per device.

v0:
```python
import math
import jax
import jax.numpy as jnp
from jax import lax
from jax.sharding import PartitionSpec as P

NG = 36
GRID = 46656


def shifted(array, axis, by):
    length = lax.axis_size(axis)
    return lax.ppermute(array, axis, [(i, (i + by) % length) for i in range(length)])


def dft_matrix(direction):
    points = jnp.arange(NG, dtype=jnp.int32)
    phases = points[:, None] * points[None, :] % NG
    angles = 2.0 * math.pi / NG * phases.astype(jnp.float32)
    cosine = jnp.cos(angles)
    sine = direction * jnp.sin(angles)
    blocks = jnp.stack([jnp.stack([cosine, sine]), jnp.stack([-sine, cosine])])
    return jnp.transpose(blocks, (0, 2, 1, 3)).astype(jnp.bfloat16)


def transform(values, matrix, keep_float):
    count = values.shape[0]
    current = values.reshape(count, 2, NG, NG * NG)
    product = jnp.einsum("uavb,pvbc->puac", matrix, current, preferred_element_type=jnp.float32)
    current = product.astype(jnp.bfloat16).reshape(count, 2, NG, NG, NG)
    product = jnp.einsum("uavb,pvxbz->puxaz", matrix, current, preferred_element_type=jnp.float32)
    current = product.astype(jnp.bfloat16)
    product = jnp.einsum("uavb,pvxyb->puxya", matrix, current, preferred_element_type=jnp.float32)
    if not keep_float:
        product = product.astype(jnp.bfloat16)
    return product.reshape(count, 2, NG * NG * NG)


def add_block(
    accum_real,
    accum_imag,
    local_bands,
    visiting,
    visiting_occ,
    kernel,
    forward_matrix,
    inverse_matrix,
):
    c = local_bands[:, 0].astype(jnp.float32)[None]
    d = local_bands[:, 1].astype(jnp.float32)[None]
    a = visiting[:, 0].astype(jnp.float32)[:, None]
    b = visiting[:, 1].astype(jnp.float32)[:, None]
    visits = visiting.shape[0]
    owned = local_bands.shape[0]
    density = jnp.stack([a * c + b * d, a * d - b * c], axis=2).astype(jnp.bfloat16)
    density = density.reshape(visits * owned, 2, density.shape[3])
    spectrum = transform(density, forward_matrix, False)
    screened = (spectrum.astype(jnp.float32) * (kernel / GRID)).astype(jnp.bfloat16)
    potential = transform(screened, inverse_matrix, True)
    potential = potential.reshape(visits, owned, 2, potential.shape[2])
    weight = (-0.5 * visiting_occ.astype(jnp.float32))[:, None, None]
    e = potential[:, :, 0]
    f = potential[:, :, 1]
    accum_real = accum_real + jnp.sum(weight * (a * e - b * f), axis=0)
    accum_imag = accum_imag + jnp.sum(weight * (a * f + b * e), axis=0)
    return (accum_real, accum_imag)


def contract(x, y):
    return jnp.einsum("ig,jg->ij", x, y, preferred_element_type=jnp.float32)


def gram_block(bra_rows, ket_rows):
    c = bra_rows[:, 0]
    d = bra_rows[:, 1]
    e = ket_rows[:, 0]
    f = ket_rows[:, 1]
    real_part = contract(c, e) + contract(d, f)
    imag_part = contract(c, f) - contract(d, e)
    return jnp.stack([real_part, imag_part])


def shards(orbitals, occupation, kernel):
    local_bands = orbitals[0]
    own_occupation = occupation[0]
    forward_matrix = dft_matrix(1.0)
    inverse_matrix = dft_matrix(-1.0)
    zeros_grid = jnp.zeros((local_bands.shape[0], local_bands.shape[2]), jnp.float32)
    first_block, first_occ = shifted((local_bands, own_occupation), "pool", 1)
    accum_real, accum_imag = add_block(
        zeros_grid,
        zeros_grid,
        local_bands,
        first_block,
        first_occ,
        kernel,
        forward_matrix,
        inverse_matrix,
    )
    second_block, second_occ = shifted((first_block, first_occ), "band", 1)
    accum_real, accum_imag = add_block(
        accum_real,
        accum_imag,
        local_bands,
        second_block,
        second_occ,
        kernel,
        forward_matrix,
        inverse_matrix,
    )
    exchanged = jnp.stack([accum_real, accum_imag], axis=1).astype(jnp.bfloat16)
    norm_factor = 1.0 / math.sqrt(GRID)
    part = (
        gram_block(lax.all_gather(local_bands, "band", axis=0, tiled=True), exchanged) * norm_factor
    )
    return (exchanged[None], part[None])


def solution(mesh):
    return jax.shard_map(
        shards,
        mesh=mesh,
        in_specs=(P("pool", "band", None, None), P("pool", "band"), P()),
        out_specs=(P("pool", "band", None, None), P("pool", None, None, "band")),
        check_vma=False,
    )
```

profile of v0, /device:TPU:1, one launch (start us, length us, event | category | flops | bytes accessed | tf_op | source)
XLA Modules:
  0.0 71.4 jit_solution(13063176755829954966)
XLA Ops:
  7.2 0.7 all-gather.3.cloned.1.call-update
  7.9 5.6 %collective-permute-start.1 = (bf16[1,2,46656]{2,1,0:T(2,128)(2,1)}, bf16[1,2,46656]{2,1,0:T(2,128)(2,1)S(1)}, u32[]{:S(2)}, u32[]{:S(2)}) collective-permute-start(bf16[1,2,46656]{2,1,0:T(2,128)(2,1)} %bitcast.325), channel_id=1, source_target_pairs={{0,16},{16,32},{32,48},{48,64},{64,80},{80,96},{96,112},{112,128},... | collective-permute-start | bytes 559880 | tf_op jit(solution)/shard_map/ppermute | solution.py:13
  13.5 3.3 %collective-permute-start = (s32[1]{0:T(128)}, s32[1]{0:T(128)}, u32[]{:S(2)}, u32[]{:S(2)}) collective-permute-start(s32[1]{0:T(128)} %bitcast), channel_id=1, source_target_pairs={{0,16},{16,32},{32,48},{48,64},{64,80},{80,96},{96,112},{112,128},... | collective-permute-start | bytes 20 | tf_op jit(solution)/shard_map/ppermute | solution.py:13
  16.9 0.9 %broadcast_multiply_fusion = f32[46656]{0:T(1024)S(1)} fusion(f32[46656]{0:T(1024)} %param.5), kind=kLoop, calls=%fused_computation.86 | loop fusion | flops 46656 | bytes 373248 | tf_op jit(solution)/shard_map/div | solution.py:58
  18.2 8.9 %collective-permute-done.1 = bf16[1,2,46656]{2,1,0:T(2,128)(2,1)S(1)} collective-permute-done((bf16[1,2,46656]{2,1,0:T(2,128)(2,1)}, bf16[1,2,46656]{2,1,0:T(2,128)(2,1)S(1)}, u32[]{:S(2)}, u32[]{:S(2)}) %collective-permute-start.1) | collective-permute-done | bytes 186656 | tf_op jit(solution)/shard_map/ppermute | solution.py:13
  27.1 4.2 %collective-permute-start.3 = (bf16[1,2,46656]{2,1,0:T(2,128)(2,1)S(1)}, bf16[1,2,46656]{2,1,0:T(2,128)(2,1)S(1)}, u32[]{:S(2)}, u32[]{:S(2)}) collective-permute-start(bf16[1,2,46656]{2,1,0:T(2,128)(2,1)S(1)} %collective-permute-done.1), channel_id=1, source_target_pairs={{0,1},{1,2},{2,3},{3,4},{4,5},{5,6},{6,7},{7,8},{8,9},{9,10},{10,1... | collective-permute-start | bytes 559880 | tf_op jit(solution)/shard_map/ppermute | solution.py:13
  32.2 1.9 %collective-permute-start.2 = (s32[1]{0:T(128)}, s32[1]{0:T(128)}, u32[]{:S(2)}, u32[]{:S(2)}) collective-permute-start(s32[1]{0:T(128)} %collective-permute-done), channel_id=1, source_target_pairs={{0,1},{1,2},{2,3},{3,4},{4,5},{5,6},{6,7},{7,8},{8,9},{9,10},{10,1... | collective-permute-start | bytes 20 | tf_op jit(solution)/shard_map/ppermute | solution.py:13
  34.1 1.7 %collective-permute-done.2 = s32[1]{0:T(128)} collective-permute-done((s32[1]{0:T(128)}, s32[1]{0:T(128)}, u32[]{:S(2)}, u32[]{:S(2)}) %collective-permute-start.2) | collective-permute-done | bytes 36 | tf_op jit(solution)/shard_map/ppermute | solution.py:13
  36.4 3.8 %convert_reduce_fusion.1 = (bf16[46656]{0:T(1024)(128)(2,1)S(1)}, bf16[46656]{0:T(1024)(128)(2,1)S(1)}, bf16[46656]{0:T(1024)(128)(2,1)S(1)}, bf16[46656]{0:T(1024)(128)(2,1)S(1)}) fusion(bf16[1,2,46656]{2,1,0:T(2,128)(2,1)} %bitcast.326, bf16[1,2,46656]{2,1,0:T(2,128)(2,1)S(1)} %collective-permute-done.3, bf16[1,2,46656]{2,1,0:T(2,128)(2,1)S(1)} %collective-permute-done.1), kind=kLoop, calls=%fused_computation.83 | loop fusion | flops 1026432 | bytes 933120 | tf_op jit(solution)/shard_map/convert.15
  40.5 0.3 fusion.7
  40.8 0.6 reshape.535
  41.4 0.9 %convert_bitcast_fusion.1 = f32[1,2,36,36,36]{4,3,1,2,0:T(8,128)S(1)} fusion(bf16[1,2,36,36]{3,2,1,0:T(8,128)(2,1)S(1)} %get-tuple-element.14, bf16[1,2,36,36]{3,2,1,0:T(8,128)(2,1)S(1)} %get-tuple-element.15, bf16[2,36,36,36]{3,2,1,0:T(8,128)(2,1)S(1)} %reshape.535), kind=kOutput, calls=%fused_computation.16 | convolution fusion | flops 27195264 | bytes 570240 | tf_op jit(solution)/shard_map/uavb,pvxyb->puxya/dot_general | solution.py:33
  42.3 1.1 %reshape.496 = f32[2,36,1296]{2,0,1:T(2,128)S(1)} reshape(f32[1,2,36,36,36]{4,3,1,2,0:T(8,128)S(1)} %convert_bitcast_fusion.1) | data formatting | bytes 746496 | tf_op jit(solution)/shard_map/convert_element_type | solution.py:58
  44.0 0.6 reshape.537
  44.6 0.9 %convert_bitcast_fusion = f32[1,2,36,36,36]{4,3,1,2,0:T(8,128)S(1)} fusion(bf16[1,2,36,36]{3,2,1,0:T(8,128)(2,1)S(1)} %get-tuple-element.14, bf16[1,2,36,36]{3,2,1,0:T(8,128)(2,1)S(1)} %get-tuple-element.15, bf16[2,36,36,36]{3,2,1,0:T(8,128)(2,1)S(1)} %reshape.537), kind=kOutput, calls=%fused_computation.15 | convolution fusion | flops 27195264 | bytes 570240 | tf_op jit(solution)/shard_map/uavb,pvxyb->puxya/dot_general | solution.py:33
  45.5 1.1 %reshape.497 = f32[2,36,1296]{2,0,1:T(2,128)S(1)} reshape(f32[1,2,36,36,36]{4,3,1,2,0:T(8,128)S(1)} %convert_bitcast_fusion) | data formatting | bytes 746496 | tf_op jit(solution)/shard_map/convert_element_type | solution.py:58
  46.5 1.0 %multiply_convert_fusion = (bf16[2,36,1296]{2,0,1:T(2,128)(2,1)S(1)}, bf16[2,36,1296]{2,0,1:T(2,128)(2,1)}) fusion(f32[2,36,1296]{2,0,1:T(2,128)S(1)} %reshape.497, f32[36,1296]{1,0:T(8,128)S(1)} %mul.321, f32[2,36,1296]{2,0,1:T(2,128)S(1)} %reshape.496), kind=kLoop, calls=%fused_computation.47 | loop fusion | flops 373248 | bytes 1306368 | tf_op jit(solution)/shard_map/convert_element_type | solution.py:58
  47.8 0.6 reshape.538
  48.5 0.9 %convolution_bitcast_fusion.4 = f32[1,2,36,36,36]{4,3,1,2,0:T(8,128)S(1)} fusion(bf16[1,2,36,36]{3,2,1,0:T(8,128)(2,1)S(1)} %get-tuple-element.13, bf16[1,2,36,36]{3,2,1,0:T(8,128)(2,1)S(1)} %get-tuple-element.12, bf16[2,36,36,36]{3,2,1,0:T(8,128)(2,1)S(1)} %reshape.538), kind=kOutput, calls=%fused_computation.23 | convolution fusion | flops 27008640 | bytes 570240 | tf_op jit(solution)/shard_map/uavb,pvxyb->puxya/dot_general | solution.py:33
  49.5 1.7 %reshape_reshape.9 = f32[1,1,2,46656]{3,2,1,0:T(2,128)} reshape(f32[1,2,36,36,36]{4,3,2,1,0:T(8,128)S(1)} %copy.47) | data formatting | bytes 746496 | tf_op jit(solution)/shard_map/reshape;reshape | solution.py:60
  51.5 0.8 %reshape.536 = bf16[2,36,36,36]{3,2,1,0:T(8,128)(2,1)S(1)} reshape(bf16[1,2,36,1296]{3,2,1,0:T(8,128)(2,1)S(1)} %fusion.6) | data formatting | bytes 373248 | tf_op jit(solution)/shard_map/reshape.20
  52.3 0.9 %convolution_bitcast_fusion.5 = f32[1,2,36,36,36]{4,3,1,2,0:T(8,128)S(1)} fusion(bf16[1,2,36,36]{3,2,1,0:T(8,128)(2,1)S(1)} %get-tuple-element.13, bf16[1,2,36,36]{3,2,1,0:T(8,128)(2,1)S(1)} %get-tuple-element.12, bf16[2,36,36,36]{3,2,1,0:T(8,128)(2,1)S(1)} %reshape.536), kind=kOutput, calls=%fused_computation.24 | convolution fusion | flops 27008640 | bytes 570240 | tf_op jit(solution)/shard_map/uavb,pvxyb->puxya/dot_general | solution.py:33
  53.3 1.0 %reshape_reshape.8 = f32[1,1,2,46656]{3,2,1,0:T(2,128)S(1)} reshape(f32[1,2,36,36,36]{4,3,2,1,0:T(8,128)S(1)} %copy.39) | data formatting | bytes 746496 | tf_op jit(solution)/shard_map/reshape;reshape | solution.py:60
  54.2 1.5 %multiply_add_fusion.1 = (bf16[1,1,46656]{2,1,0:T(2,128)(2,1)S(1)}, bf16[1,1,46656]{2,1,0:T(2,128)(2,1)S(1)}) fusion(f32[1,1,2,46656]{3,2,1,0:T(2,128)S(1)} %reshape_reshape.8, f32[1,1,2,46656]{3,2,1,0:T(2,128)S(1)} %copy-done, f32[]{:T(128)} %bitcast.45, f32[]{:T(128)} %bitcast.1, bf16[1,2,46656]{2,1,0:T(2,128)(2,1)S(1)} %collective-permute-done.1, ...), kind=kLoop, calls=%fused_computation.81 | loop fusion | flops 1119744 | bytes 1306376 | tf_op jit(solution)/shard_map/add | solution.py:64
  55.7 1.1 %pad_maximum_fusion = bf16[1,1,2,46656]{3,2,1,0:T(2,128)(2,1)} fusion(bf16[1,1,1,46656]{3,2,1,0:T(2,128)(2,1)S(1)} %bitcast.327, bf16[1,1,1,46656]{3,2,1,0:T(2,128)(2,1)S(1)} %bitcast.328), kind=kLoop, calls=%fused_computation.69 | loop fusion | flops 373248 | bytes 373248 | tf_op jit(solution)/shard_map/stack | solution.py:111
  56.8 2.9 %all-gather.3.cloned.1.call-done = bf16[16,1,2,46656]{3,2,1,0:T(2,128)(2,1)} async-done(((bf16[1,1,2,46656]{3,2,1,0:T(2,128)(2,1)}), bf16[16,1,2,46656]{3,2,1,0:T(2,128)(2,1)}) %all-gather.3.cloned.1.call-update) | async-done | bytes 2986000 | tf_op jit(solution)/shard_map/all_gather | solution.py:114
  59.7 2.1 %copy.118 = bf16[16,1,2,46656]{3,0,2,1:T(8,128)(2,1)S(1)} copy(bf16[16,1,2,46656]{3,2,1,0:T(2,128)(2,1)} %all-gather.3.cloned.1.call-done) | data formatting | bytes 5971968 | tf_op jit(solution)/shard_map/all_gather | solution.py:114
  61.8 0.5 fusion.18
  62.3 0.6 fusion.19
  62.9 0.5 fusion.25
  63.4 0.5 fusion.23
  64.0 0.6 maximum_multiply_fusion
  (21 shorter events, 2.2 us)
Async XLA Ops:
  7.2 52.5 %all-gather.3.cloned.1.call-start = ((), (), s32[]{:S(2)}) async-start(), calls=%async_computation | async-start | bytes 3176960 | tf_op jit(solution)/shard_map/all_gather | solution.py:114
  7.9 19.2 %collective-permute-start.1 = (bf16[1,2,46656]{2,1,0:T(2,128)(2,1)}, bf16[1,2,46656]{2,1,0:T(2,128)(2,1)S(1)}, u32[]{:S(2)}, u32[]{:S(2)}) collective-permute-start(bf16[1,2,46656]{2,1,0:T(2,128)(2,1)} %bitcast.325), channel_id=1, source_target_pairs={{0,16},{16,32},{32,48},{48,64},{64,80},{80,96},{96,112},{112,128},... | collective-permute-start | bytes 559880 | tf_op jit(solution)/shard_map/ppermute | solution.py:13
  13.5 17.9 %collective-permute-start = (s32[1]{0:T(128)}, s32[1]{0:T(128)}, u32[]{:S(2)}, u32[]{:S(2)}) collective-permute-start(s32[1]{0:T(128)} %bitcast), channel_id=1, source_target_pairs={{0,16},{16,32},{32,48},{48,64},{64,80},{80,96},{96,112},{112,128},... | collective-permute-start | bytes 20 | tf_op jit(solution)/shard_map/ppermute | solution.py:13
  27.1 9.3 %collective-permute-start.3 = (bf16[1,2,46656]{2,1,0:T(2,128)(2,1)S(1)}, bf16[1,2,46656]{2,1,0:T(2,128)(2,1)S(1)}, u32[]{:S(2)}, u32[]{:S(2)}) collective-permute-start(bf16[1,2,46656]{2,1,0:T(2,128)(2,1)S(1)} %collective-permute-done.1), channel_id=1, source_target_pairs={{0,1},{1,2},{2,3},{3,4},{4,5},{5,6},{6,7},{7,8},{8,9},{9,10},{10,1... | collective-permute-start | bytes 559880 | tf_op jit(solution)/shard_map/ppermute | solution.py:13
  32.2 3.6 %collective-permute-start.2 = (s32[1]{0:T(128)}, s32[1]{0:T(128)}, u32[]{:S(2)}, u32[]{:S(2)}) collective-permute-start(s32[1]{0:T(128)} %collective-permute-done), channel_id=1, source_target_pairs={{0,1},{1,2},{2,3},{3,4},{4,5},{5,6},{6,7},{7,8},{8,9},{9,10},{10,1... | collective-permute-start | bytes 20 | tf_op jit(solution)/shard_map/ppermute | solution.py:13
  49.4 1.7 %copy-start.1 = (bf16[2,36,1296]{2,0,1:T(2,128)(2,1)S(1)}, bf16[2,36,1296]{2,0,1:T(2,128)(2,1)}, u32[]{:S(2)}) copy-start(bf16[2,36,1296]{2,0,1:T(2,128)(2,1)} %get-tuple-element.11) | copy-start | bytes 559876
  53.2 1.0 %copy-start = (f32[1,1,2,46656]{3,2,1,0:T(2,128)S(1)}, f32[1,1,2,46656]{3,2,1,0:T(2,128)}, u32[]{:S(2)}) copy-start(f32[1,1,2,46656]{3,2,1,0:T(2,128)} %reshape_reshape.9) | copy-start | bytes 1119748
Sparse Core Ops, SparseCore 0:
  10.1 49.5 all-gather.2
where the time goes:
time: 71.7 us; the launch traced here: 71.4 us
  between operations  15.5 us (22%)
  starting transfers between devices  15.2 us (21%)
  waiting for transfers between devices  14.1 us (20%)
  local copies, waits for them, and re-layouts  10.6 us (15%)
  other arithmetic  9.25 us (13%)
  matrix products  6.74 us (9%)
    ppermute x4, starting transfers between devices, shifted(): lax.ppermute(array, axis, [(i, (i + by) % length) for i in range(length)])  15.1 us
    ppermute x4, waiting for transfers between devices, shifted(): lax.ppermute(array, axis, [(i, (i + by) % length) for i in range(length)])  10.5 us
    another operation x4, other arithmetic  4.09 us
    dot_general x4, matrix products, transform(): jnp.einsum('uavb,pvxyb->puxya', matrix, current, preferred_element_type=j...  3.56 us
    all_gather x1, waiting for transfers between devices, shards(): lax.all_gather(local_bands, 'band', axis=0, tiled=True)  2.86 us
    another operation x2, local copies, waits for them, and re-layouts, add_block(): potential = potential.reshape(visits, owned, 2, potential.shape[2])  2.7 us
    another operation x4, local copies, waits for them, and re-layouts  2.63 us
    dot_general x4, matrix products, contract(): return jnp.einsum('ig,jg->ij', x, y, preferred_element_type=jnp.float32)  2.14 us
  transfers between devices with their start and end apart: 5, of which 3 were waited for; matrix products, arithmetic and copies ran while one was open for 30% of the time, Pallas kernels for 0%

commit v1 on v0

--- a/solution.py
+++ b/solution.py
@@ -111,7 +111,14 @@
     exchanged = jnp.stack([accum_real, accum_imag], axis=1).astype(jnp.bfloat16)
     norm_factor = 1.0 / math.sqrt(GRID)
     part = (
-        gram_block(lax.all_gather(local_bands, "band", axis=0, tiled=True), exchanged) * norm_factor
+        gram_block(
+            jnp.concatenate(
+                lax.all_to_all(jnp.stack([local_bands] * lax.axis_size("band")), "band", 0, 0),
+                axis=0,
+            ),
+            exchanged,
+        )
+        * norm_factor
     )
     return (exchanged[None], part[None])
 

time: 71.7 us -> 130 us (1.81); the launches traced: 71.4 us -> 128 us
  local copies, waits for them, and re-layouts: 10.6 us -> 39 us
  waiting for transfers between devices: 14.1 us -> 32.6 us
  matrix products: 6.74 us -> 21.3 us
  between operations: 15.5 us -> 2 us
  starting transfers between devices: 15.2 us -> 21.4 us
  other arithmetic: 9.25 us -> 12 us
    ppermute x4, waiting for transfers between devices: 10.5 us -> 32.6 us  [shifted(): lax.ppermute(array, axis, [(i, (i + by) % length) for i in range(length)])]
    another operation x4 -> x5, local copies, waits for them, and re-layouts: 2.63 us -> 14 us
    dot_general x4, matrix products: 3.56 us -> 12.5 us  [transform(): jnp.einsum('uavb,pvxyb->puxya', matrix, current, preferred_element_type=j...]
    all_to_all x0 -> x1, starting transfers between devices: none -> 6.69 us  [shards(): lax.all_to_all(jnp.stack([local_bands] * lax.axis_size('band')), 'band',...]
    dot_general x4, matrix products: 1.05 us -> 6.63 us  [transform(): jnp.einsum('uavb,pvbc->puac', matrix, current, preferred_element_type=jnp...]
    transpose x2, local copies, waits for them, and re-layouts: 0.19 us -> 5.28 us  [transform(): jnp.einsum('uavb,pvxyb->puxya', matrix, current, preferred_element_type=j...]
    another operation x4, local copies, waits for them, and re-layouts: 0.7 us -> 5.31 us  [add_block(): jnp.stack([a * c + b * d, a * d - b * c], axis=2).astype(jnp.bfloat16)]
    convert_element_type x2, local copies, waits for them, and re-layouts: 2.1 us -> 6.14 us  [add_block(): spectrum.astype(jnp.float32) * (kernel / GRID)]
  transfers between devices with their start and end apart: 5 -> 5, of which waited for: 3 -> 1; matrix products, arithmetic and copies ran while one was open for 30% -> 53% of each run, Pallas kernels for 0% -> 0%
where the time goes in v1:
time: 130 us; the launch traced here: 128 us
  local copies, waits for them, and re-layouts  39 us (30%)
  waiting for transfers between devices  32.6 us (25%)
  starting transfers between devices  21.4 us (16%)
  matrix products  21.3 us (16%)
  other arithmetic  12 us (9%)
  between operations  2 us (2%)
    ppermute x4, waiting for transfers between devices, shifted(): lax.ppermute(array, axis, [(i, (i + by) % length) for i in range(length)])  32.6 us
    ppermute x4, starting transfers between devices, shifted(): lax.ppermute(array, axis, [(i, (i + by) % length) for i in range(length)])  14.7 us
    dot_general x4, matrix products, transform(): jnp.einsum('uavb,pvxyb->puxya', matrix, current, preferred_element_type=j...  12.5 us
    another operation x4, local copies, waits for them, and re-layouts  9.92 us
    all_to_all x1, starting transfers between devices, shards(): lax.all_to_all(jnp.stack([local_bands] * lax.axis_size('band')), 'band',...  6.69 us
    dot_general x4, matrix products, transform(): jnp.einsum('uavb,pvbc->puac', matrix, current, preferred_element_type=jnp...  6.63 us
    convert_element_type x2, local copies, waits for them, and re-layouts, add_block(): spectrum.astype(jnp.float32) * (kernel / GRID)  6.14 us
    another operation x2, local copies, waits for them, and re-layouts, add_block(): potential = potential.reshape(visits, owned, 2, potential.shape[2])  6.08 us
  transfers between devices with their start and end apart: 5, of which 1 were waited for; matrix products, arithmetic and copies ran while one was open for 53% of the time, Pallas kernels for 0%

profile of v1, /device:TPU:1, one launch (start us, length us, event | category | flops | bytes accessed | tf_op | source)
XLA Modules:
  0.0 128.4 jit_solution(11259550441593405712)
XLA Ops:
  0.6 5.6 %collective-permute-start.1 = (bf16[1,2,46656]{2,1,0:T(2,128)(2,1)}, bf16[1,2,46656]{2,1,0:T(2,128)(2,1)S(1)}, u32[]{:S(2)}, u32[]{:S(2)}) collective-permute-start(bf16[1,2,46656]{2,1,0:T(2,128)(2,1)} %bitcast.326), channel_id=1, source_target_pairs={{0,16},{16,32},{32,48},{48,64},{64,80},{80,96},{96,112},{112,128},... | collective-permute-start | bytes 559880 | tf_op jit(solution)/shard_map/ppermute | solution.py:13
  6.3 3.3 %collective-permute-start = (s32[1]{0:T(128)}, s32[1]{0:T(128)}, u32[]{:S(2)}, u32[]{:S(2)}) collective-permute-start(s32[1]{0:T(128)} %bitcast), channel_id=1, source_target_pairs={{0,16},{16,32},{32,48},{48,64},{64,80},{80,96},{96,112},{112,128},... | collective-permute-start | bytes 20 | tf_op jit(solution)/shard_map/ppermute | solution.py:13
  9.6 4.1 %stack.106 = bf16[16,1,2,46656]{3,2,1,0:T(2,128)(2,1)} broadcast(bf16[2,46656]{1,0:T(2,128)(2,1)} %bitcast.327), dimensions={2,3} | broadcast | bytes 3172608 | tf_op jit(solution)/shard_map/stack | solution.py:116
  13.7 6.7 %all-to-all-start = ((bf16[16,1,2,46656]{3,2,1,0:T(2,128)(2,1)}), bf16[16,1,2,46656]{3,2,1,0:T(2,128)(2,1)S(1)}, u32[]{:S(2)}, u32[]{:S(2)}) async-start(bf16[16,1,2,46656]{3,2,1,0:T(2,128)(2,1)} %stack.106), calls=%async_computation | async-start | bytes 5980160 | tf_op jit(solution)/shard_map/all_to_all | solution.py:116
  22.4 3.5 %collective-permute-start.3 = (bf16[1,2,46656]{2,1,0:T(2,128)(2,1)S(1)}, bf16[1,2,46656]{2,1,0:T(2,128)(2,1)S(1)}, u32[]{:S(2)}, u32[]{:S(2)}) collective-permute-start(bf16[1,2,46656]{2,1,0:T(2,128)(2,1)S(1)} %collective-permute-done.1), channel_id=1, source_target_pairs={{0,1},{1,2},{2,3},{3,4},{4,5},{5,6},{6,7},{7,8},{8,9},{9,10},{10,1... | collective-permute-start | bytes 559880 | tf_op jit(solution)/shard_map/ppermute | solution.py:13
  27.3 2.2 %collective-permute-start.2 = (s32[1]{0:T(128)}, s32[1]{0:T(128)}, u32[]{:S(2)}, u32[]{:S(2)}) collective-permute-start(s32[1]{0:T(128)} %collective-permute-done), channel_id=1, source_target_pairs={{0,1},{1,2},{2,3},{3,4},{4,5},{5,6},{6,7},{7,8},{8,9},{9,10},{10,1... | collective-permute-start | bytes 20 | tf_op jit(solution)/shard_map/ppermute | solution.py:13
  29.6 32.6 %collective-permute-done.2 = s32[1]{0:T(128)} collective-permute-done((s32[1]{0:T(128)}, s32[1]{0:T(128)}, u32[]{:S(2)}, u32[]{:S(2)}) %collective-permute-start.2) | collective-permute-done | bytes 36 | tf_op jit(solution)/shard_map/ppermute | solution.py:13
  62.8 3.4 %convert_reduce_fusion.1 = (bf16[46656]{0:T(1024)(128)(2,1)}, bf16[46656]{0:T(1024)(128)(2,1)}, bf16[46656]{0:T(1024)(128)(2,1)}, bf16[46656]{0:T(1024)(128)(2,1)}) fusion(bf16[1,2,46656]{2,1,0:T(2,128)(2,1)S(1)} %bitcast.328, bf16[1,2,46656]{2,1,0:T(2,128)(2,1)S(1)} %collective-permute-done.3, bf16[1,2,46656]{2,1,0:T(2,128)(2,1)S(1)} %collective-permute-done.1), kind=kLoop, calls=%fused_computation.83 | loop fusion | flops 1026432 | bytes 933120 | tf_op jit(solution)/shard_map/convert.15
  66.2 1.1 stack.87
  67.3 1.7 %stack.88 = bf16[1,36,1296]{2,1,0:T(8,128)(2,1)} reshape(bf16[46656]{0:T(1024)(128)(2,1)} %get-tuple-element.6) | data formatting | bytes 186624 | tf_op jit(solution)/shard_map/stack | solution.py:55
  69.0 1.9 %fusion.7 = bf16[1,2,36,1296]{3,2,1,0:T(8,128)(2,1)} fusion(bf16[1,36,1296]{2,1,0:T(8,128)(2,1)} %stack.88, bf16[1,36,1296]{2,1,0:T(8,128)(2,1)S(1)} %stack.87, bf16[1,2,36,36]{3,2,1,0:T(8,128)(2,1)} %get-tuple-element.14, bf16[1,2,36,36]{3,2,1,0:T(8,128)(2,1)} %get-tuple-element.15), kind=kOutput, calls=%fused_computation.12 | convolution fusion | flops 13924224 | bytes 383616 | tf_op jit(solution)/shard_map/uavb,pvbc->puac/dot_general | solution.py:29
  70.9 2.4 %reshape.541 = bf16[2,36,36,36]{3,2,1,0:T(8,128)(2,1)} reshape(bf16[1,2,36,1296]{3,2,1,0:T(8,128)(2,1)} %fusion.7) | data formatting | bytes 373248 | tf_op jit(solution)/shard_map/reshape.3
  73.3 3.2 %convert_bitcast_fusion.1 = f32[1,2,36,36,36]{4,3,1,2,0:T(8,128)} fusion(bf16[1,2,36,36]{3,2,1,0:T(8,128)(2,1)} %get-tuple-element.14, bf16[1,2,36,36]{3,2,1,0:T(8,128)(2,1)} %get-tuple-element.15, bf16[2,36,36,36]{3,2,1,0:T(8,128)(2,1)} %reshape.541), kind=kOutput, calls=%fused_computation.16 | convolution fusion | flops 27195264 | bytes 570240 | tf_op jit(solution)/shard_map/uavb,pvxyb->puxya/dot_general | solution.py:33
  76.5 3.1 %reshape.503 = f32[2,36,1296]{2,0,1:T(2,128)} reshape(f32[1,2,36,36,36]{4,3,1,2,0:T(8,128)} %convert_bitcast_fusion.1) | data formatting | bytes 746496 | tf_op jit(solution)/shard_map/convert_element_type | solution.py:58
  79.5 1.7 %stack.100 = bf16[1,36,1296]{2,1,0:T(8,128)(2,1)} reshape(bf16[46656]{0:T(1024)(128)(2,1)} %get-tuple-element.2) | data formatting | bytes 186624 | tf_op jit(solution)/shard_map/stack | solution.py:55
  82.1 1.9 %fusion.5 = bf16[1,2,36,1296]{3,2,1,0:T(8,128)(2,1)} fusion(bf16[1,36,1296]{2,1,0:T(8,128)(2,1)} %stack.101, bf16[1,36,1296]{2,1,0:T(8,128)(2,1)} %stack.100, bf16[1,2,36,36]{3,2,1,0:T(8,128)(2,1)S(1)} %copy-done.5, bf16[1,2,36,36]{3,2,1,0:T(8,128)(2,1)S(1)} %copy-done.6), kind=kOutput, calls=%fused_computation.10 | convolution fusion | flops 13924224 | bytes 383616 | tf_op jit(solution)/shard_map/uavb,pvbc->puac/dot_general | solution.py:29
  84.0 2.4 %reshape.543 = bf16[2,36,36,36]{3,2,1,0:T(8,128)(2,1)} reshape(bf16[1,2,36,1296]{3,2,1,0:T(8,128)(2,1)} %fusion.5) | data formatting | bytes 373248 | tf_op jit(solution)/shard_map/reshape.29
  86.4 3.1 %convert_bitcast_fusion = f32[1,2,36,36,36]{4,3,1,2,0:T(8,128)} fusion(bf16[1,2,36,36]{3,2,1,0:T(8,128)(2,1)S(1)} %copy-done.5, bf16[1,2,36,36]{3,2,1,0:T(8,128)(2,1)S(1)} %copy-done.6, bf16[2,36,36,36]{3,2,1,0:T(8,128)(2,1)} %reshape.543), kind=kOutput, calls=%fused_computation.15 | convolution fusion | flops 27195264 | bytes 570240 | tf_op jit(solution)/shard_map/uavb,pvxyb->puxya/dot_general | solution.py:33
  89.6 3.1 %reshape.504 = f32[2,36,1296]{2,0,1:T(2,128)} reshape(f32[1,2,36,36,36]{4,3,1,2,0:T(8,128)} %convert_bitcast_fusion) | data formatting | bytes 746496 | tf_op jit(solution)/shard_map/convert_element_type | solution.py:58
  92.6 2.3 %multiply_convert_fusion = (bf16[2,36,1296]{2,0,1:T(2,128)(2,1)S(1)}, bf16[2,36,1296]{2,0,1:T(2,128)(2,1)}) fusion(f32[2,36,1296]{2,0,1:T(2,128)} %reshape.504, f32[36,1296]{1,0:T(8,128)} %mul.321, f32[2,36,1296]{2,0,1:T(2,128)} %reshape.503), kind=kLoop, calls=%fused_computation.47 | loop fusion | flops 373248 | bytes 1306368 | tf_op jit(solution)/shard_map/convert_element_type | solution.py:58
  94.9 1.0 fusion.4
  95.9 2.4 %reshape.544 = bf16[2,36,36,36]{3,2,1,0:T(8,128)(2,1)} reshape(bf16[1,2,36,1296]{3,2,1,0:T(8,128)(2,1)} %fusion.4) | data formatting | bytes 373248 | tf_op jit(solution)/shard_map/reshape.36
  98.3 3.1 %convolution_bitcast_fusion.4 = f32[1,2,36,36,36]{4,3,1,2,0:T(8,128)} fusion(bf16[1,2,36,36]{3,2,1,0:T(8,128)(2,1)S(1)} %copy-done.2, bf16[1,2,36,36]{3,2,1,0:T(8,128)(2,1)S(1)} %copy-done.1, bf16[2,36,36,36]{3,2,1,0:T(8,128)(2,1)} %reshape.544), kind=kOutput, calls=%fused_computation.23 | convolution fusion | flops 27008640 | bytes 570240 | tf_op jit(solution)/shard_map/uavb,pvxyb->puxya/dot_general | solution.py:33
  101.4 2.6 %copy.46 = f32[1,2,36,36,36]{4,3,2,1,0:T(8,128)} copy(f32[1,2,36,36,36]{4,3,1,2,0:T(8,128)} %convolution_bitcast_fusion.4) | data formatting | bytes 746496 | tf_op jit(solution)/shard_map/uavb,pvxyb->puxya/transpose | solution.py:33
  104.0 3.0 %reshape_reshape.9 = f32[1,1,2,46656]{3,2,1,0:T(2,128)} reshape(f32[1,2,36,36,36]{4,3,2,1,0:T(8,128)} %copy.46) | data formatting | bytes 746496 | tf_op jit(solution)/shard_map/reshape;reshape | solution.py:60
  107.1 1.9 %fusion.6 = bf16[1,2,36,1296]{3,2,1,0:T(8,128)(2,1)} fusion(bf16[2,36,1296]{2,0,1:T(2,128)(2,1)} %get-tuple-element.11, bf16[1,2,36,36]{3,2,1,0:T(8,128)(2,1)S(1)} %copy-done.2, bf16[1,2,36,36]{3,2,1,0:T(8,128)(2,1)S(1)} %copy-done.1), kind=kOutput, calls=%fused_computation.11 | convolution fusion | flops 13550976 | bytes 383616 | tf_op jit(solution)/shard_map/uavb,pvbc->puac/dot_general | solution.py:29
  109.0 2.6 %reshape.542 = bf16[2,36,36,36]{3,2,1,0:T(8,128)(2,1)} reshape(bf16[1,2,36,1296]{3,2,1,0:T(8,128)(2,1)} %fusion.6) | data formatting | bytes 373248 | tf_op jit(solution)/shard_map/reshape.19
  111.6 3.1 %convolution_bitcast_fusion.5 = f32[1,2,36,36,36]{4,3,1,2,0:T(8,128)} fusion(bf16[1,2,36,36]{3,2,1,0:T(8,128)(2,1)S(1)} %copy-done.2, bf16[1,2,36,36]{3,2,1,0:T(8,128)(2,1)S(1)} %copy-done.1, bf16[2,36,36,36]{3,2,1,0:T(8,128)(2,1)} %reshape.542), kind=kOutput, calls=%fused_computation.24 | convolution fusion | flops 27008640 | bytes 570240 | tf_op jit(solution)/shard_map/uavb,pvxyb->puxya/dot_general | solution.py:33
  114.7 2.6 %copy.38 = f32[1,2,36,36,36]{4,3,2,1,0:T(8,128)} copy(f32[1,2,36,36,36]{4,3,1,2,0:T(8,128)} %convolution_bitcast_fusion.5) | data formatting | bytes 746496 | tf_op jit(solution)/shard_map/uavb,pvxyb->puxya/transpose | solution.py:33
  117.4 3.0 %reshape_reshape.8 = f32[1,1,2,46656]{3,2,1,0:T(2,128)} reshape(f32[1,2,36,36,36]{4,3,2,1,0:T(8,128)} %copy.38) | data formatting | bytes 746496 | tf_op jit(solution)/shard_map/reshape;reshape | solution.py:60
  120.4 2.8 %multiply_add_fusion.1 = (bf16[1,1,46656]{2,1,0:T(2,128)(2,1)S(1)}, bf16[1,1,46656]{2,1,0:T(2,128)(2,1)S(1)}) fusion(f32[1,1,2,46656]{3,2,1,0:T(2,128)} %reshape_reshape.8, f32[1,1,2,46656]{3,2,1,0:T(2,128)} %reshape_reshape.9, f32[]{:T(128)} %bitcast.45, f32[]{:T(128)} %bitcast.1, bf16[1,2,46656]{2,1,0:T(2,128)(2,1)S(1)} %collective-permute-done.1, ...), kind=kLoop, calls=%fused_computation.81 | loop fusion | flops 1119744 | bytes 1306376 | tf_op jit(solution)/shard_map/add | solution.py:64
  123.9 1.1 pad_maximum_fusion
  (33 shorter events, 7.7 us)
Async XLA Ops:
  0.6 21.8 %collective-permute-start.1 = (bf16[1,2,46656]{2,1,0:T(2,128)(2,1)}, bf16[1,2,46656]{2,1,0:T(2,128)(2,1)S(1)}, u32[]{:S(2)}, u32[]{:S(2)}) collective-permute-start(bf16[1,2,46656]{2,1,0:T(2,128)(2,1)} %bitcast.326), channel_id=1, source_target_pairs={{0,16},{16,32},{32,48},{48,64},{64,80},{80,96},{96,112},{112,128},... | collective-permute-start | bytes 559880 | tf_op jit(solution)/shard_map/ppermute | solution.py:13
  6.3 20.4 %collective-permute-start = (s32[1]{0:T(128)}, s32[1]{0:T(128)}, u32[]{:S(2)}, u32[]{:S(2)}) collective-permute-start(s32[1]{0:T(128)} %bitcast), channel_id=1, source_target_pairs={{0,16},{16,32},{32,48},{48,64},{64,80},{80,96},{96,112},{112,128},... | collective-permute-start | bytes 20 | tf_op jit(solution)/shard_map/ppermute | solution.py:13
  13.7 49.1 %copy-start = (bf16[1,1,2,46656]{3,2,1,0:T(2,128)(2,1)S(1)}, bf16[1,1,2,46656]{3,2,1,0:T(2,128)(2,1)}, u32[]{:S(2)}) copy-start(bf16[1,1,2,46656]{3,2,1,0:T(2,128)(2,1)} %param.3) | copy-start | bytes 559876
  13.7 111.3 %all-to-all-start = ((bf16[16,1,2,46656]{3,2,1,0:T(2,128)(2,1)}), bf16[16,1,2,46656]{3,2,1,0:T(2,128)(2,1)S(1)}, u32[]{:S(2)}, u32[]{:S(2)}) async-start(bf16[16,1,2,46656]{3,2,1,0:T(2,128)(2,1)} %stack.106), calls=%async_computation | async-start | bytes 5980160 | tf_op jit(solution)/shard_map/all_to_all | solution.py:116
  22.4 40.4 %collective-permute-start.3 = (bf16[1,2,46656]{2,1,0:T(2,128)(2,1)S(1)}, bf16[1,2,46656]{2,1,0:T(2,128)(2,1)S(1)}, u32[]{:S(2)}, u32[]{:S(2)}) collective-permute-start(bf16[1,2,46656]{2,1,0:T(2,128)(2,1)S(1)} %collective-permute-done.1), channel_id=1, source_target_pairs={{0,1},{1,2},{2,3},{3,4},{4,5},{5,6},{6,7},{7,8},{8,9},{9,10},{10,1... | collective-permute-start | bytes 559880 | tf_op jit(solution)/shard_map/ppermute | solution.py:13
  27.3 34.8 %collective-permute-start.2 = (s32[1]{0:T(128)}, s32[1]{0:T(128)}, u32[]{:S(2)}, u32[]{:S(2)}) collective-permute-start(s32[1]{0:T(128)} %collective-permute-done), channel_id=1, source_target_pairs={{0,1},{1,2},{2,3},{3,4},{4,5},{5,6},{6,7},{7,8},{8,9},{9,10},{10,1... | collective-permute-start | bytes 20 | tf_op jit(solution)/shard_map/ppermute | solution.py:13
  76.5 4.8 %copy-start.7 = (bf16[46656]{0:T(1024)(128)(2,1)S(1)}, bf16[46656]{0:T(1024)(128)(2,1)}, u32[]{:S(2)}) copy-start(bf16[46656]{0:T(1024)(128)(2,1)} %get-tuple-element.3) | copy-start | bytes 279940
  76.5 5.6 %copy-start.5 = (bf16[1,2,36,36]{3,2,1,0:T(8,128)(2,1)S(1)}, bf16[1,2,36,36]{3,2,1,0:T(8,128)(2,1)}, u32[]{:S(2)}) copy-start(bf16[1,2,36,36]{3,2,1,0:T(8,128)(2,1)} %get-tuple-element.14) | copy-start | bytes 15556
  76.5 5.6 %copy-start.6 = (bf16[1,2,36,36]{3,2,1,0:T(8,128)(2,1)S(1)}, bf16[1,2,36,36]{3,2,1,0:T(8,128)(2,1)}, u32[]{:S(2)}) copy-start(bf16[1,2,36,36]{3,2,1,0:T(8,128)(2,1)} %get-tuple-element.15) | copy-start | bytes 15556
  89.6 5.3 %copy-start.1 = (bf16[1,2,36,36]{3,2,1,0:T(8,128)(2,1)S(1)}, bf16[1,2,36,36]{3,2,1,0:T(8,128)(2,1)}, u32[]{:S(2)}) copy-start(bf16[1,2,36,36]{3,2,1,0:T(8,128)(2,1)} %get-tuple-element.12) | copy-start | bytes 15556
  89.6 5.3 %copy-start.2 = (bf16[1,2,36,36]{3,2,1,0:T(8,128)(2,1)S(1)}, bf16[1,2,36,36]{3,2,1,0:T(8,128)(2,1)}, u32[]{:S(2)}) copy-start(bf16[1,2,36,36]{3,2,1,0:T(8,128)(2,1)} %get-tuple-element.13) | copy-start | bytes 15556
  123.2 0.7 copy-start.3
  125.3 0.9 copy-start.4
